TPU v7x, 768 devices: a whole 4x8x12 slice. The times are simulated.
768 devices in a mesh: mom: 24 (over z_hi, y), trow: 4 (over z_lo), tcol: 8 (over x, core).
Axes of the slice: x: 4, y: 8, z: 12 (z_hi: 3, z_lo: 4; z = z_hi * 4 + z_lo), core: 2. Of those that a mesh axis runs over, the one named last changes fastest.
Arguments:
- g_free: float32 [2, 24, 1536, 1536], P(None, 'mom', 'tcol', 'trow'), may hold values from -6 to 6
- g_greater_t: float32 [2, 24, 1536, 1536], P(None, 'mom', 'tcol', 'trow'), may hold values from -6 to 6
- momentum_map: int32 [24], replicated, may hold values from 0 to 23, each once
- weights: float32 [1536], replicated, may hold values from 0.00076546555 to 0.0076546553
Outputs:
- g_out: float32 [2, 24, 1536, 1536], P(None, 'mom', 'tcol', 'trow')
Inputs may be any that keep to these rules, and one draw needn't show every extreme that they name: `momentum_map`: each number appears once.
All inputs are finite; a program needn't handle non-finite values.
Results may differ from a plain program's by a relative error of at most 0.00022.
Values sent between devices are 32-bit elements; how exact they have to be, the bound alone decides.
No kernel may reach another device: no remote copies, remote signals or barrier semaphores. Data moves between devices by JAX's collectives and lax.ppermute only.
A program may use at most 32 MiB of HBM per device.

v0:
```python
import math

import jax
import jax.numpy as jnp
from jax import lax
from jax.experimental import pallas as pl
from jax.experimental.pallas import tpu as pltpu
from jax.sharding import Mesh, PartitionSpec as P


ITERS = 2


CHUNKS = 2
VMEM = 24 * 1024 * 1024

LANES = 128
ROOT3_2 = math.sqrt(3.0) / 2.0


def c_add(a, b):
    return (a[0] + b[0], a[1] + b[1])


def c_sub(a, b):
    return (a[0] - b[0], a[1] - b[1])


def c_turn(a, sign):
    return (-a[1], a[0]) if sign > 0 else (a[1], -a[0])


def dft3(x0, x1, x2, sign):
    u = c_add(x1, x2)
    v = c_sub(x1, x2)
    m = (x0[0] - 0.5 * u[0], x0[1] - 0.5 * u[1])
    n = c_turn((ROOT3_2 * v[0], ROOT3_2 * v[1]), sign)
    return c_add(x0, u), c_add(m, n), c_sub(m, n)


def dft4(x, sign):
    t0, t1 = c_add(x[0], x[2]), c_sub(x[0], x[2])
    t2, t3 = c_add(x[1], x[3]), c_turn(c_sub(x[1], x[3]), sign)
    return [c_add(t0, t2), c_add(t1, t3), c_sub(t0, t2), c_sub(t1, t3)]


def dft6(x, sign):
    b = [c_add(x[m], x[m + 3]) for m in range(3)]
    c = [c_sub(x[m], x[m + 3]) for m in range(3)]
    even = dft3(b[0], b[1], b[2], sign)
    odd = dft3(c[0], (-c[1][0], -c[1][1]), c[2], sign)
    return [even[0], odd[2], even[1], odd[0], even[2], odd[1]]


def lattice_transform(x, sign):
    rows = [[None] * 6 for _ in range(4)]
    for across in range(6):
        column = dft4([x[6 * down + across] for down in range(4)], sign)
        for down in range(4):
            rows[down][across] = column[down]
    out = []
    for down in range(4):
        out.extend(dft6(rows[down], sign))
    return out


def self_energy_kernel(first, map_ref, weights_ref, field_ref, *refs):
    if first:
        sigma_ref, mirror_ref, where_ref = refs
    else:
        mirror_ref, sigma_ref, where_ref = refs
    momenta = field_ref.shape[0]
    for k in range(momenta):
        where_ref[map_ref[k]] = k
    spot = [where_ref[q] for q in range(momenta)]
    zl = lax.axis_index("zl")
    for lane in range(0, field_ref.shape[3], LANES):
        cut = pl.ds(lane, LANES)
        if first:
            mirror = lattice_transform(
                [(field_ref[k, 2, :, cut], field_ref[k, 3, :, cut]) for k in spot], -1
            )
            scale = 1.0 / (momenta * momenta)
            for r in range(momenta):
                mirror_ref[r, 0, :, cut] = mirror[r][0] * scale
                mirror_ref[r, 1, :, cut] = mirror[r][1] * scale
        space = lattice_transform(
            [(field_ref[k, 0, :, cut], field_ref[k, 1, :, cut]) for k in spot], 1
        )
        source = []
        for r in range(momenta):
            re, im = space[r]
            sq_re = re * re - im * im
            sq_im = 2.0 * re * im
            m_re, m_im = mirror_ref[r, 0, :, cut], mirror_ref[r, 1, :, cut]
            source.append((sq_re * m_re - sq_im * m_im, sq_re * m_im + sq_im * m_re))
        sigma = lattice_transform(source, -1)
        w = weights_ref[zl, :, cut]
        for q in range(momenta):
            sigma_ref[spot[q], 0, :, cut] = sigma[q][0] * w
            sigma_ref[spot[q], 1, :, cut] = sigma[q][1] * w


def self_energy(momentum_map, weights, field, mirror=None):
    first = mirror is None
    momenta, _, rows, cols = field.shape
    shape = jax.ShapeDtypeStruct((momenta, 2, rows, cols), jnp.float32)
    smem = pl.BlockSpec(memory_space=pltpu.SMEM)
    vmem = pl.BlockSpec(memory_space=pltpu.VMEM)
    ins = [momentum_map, weights, field] + ([] if first else [mirror])
    return pl.pallas_call(
        lambda *refs: self_energy_kernel(first, *refs),
        out_shape=(shape, shape) if first else shape,
        in_specs=[smem] + [vmem] * (len(ins) - 1),
        out_specs=(vmem, vmem) if first else vmem,
        scratch_shapes=[pltpu.SMEM((momenta,), jnp.int32)],
        compiler_params=pltpu.CompilerParams(vmem_limit_bytes=VMEM),
        name="self_energy_first" if first else "self_energy_next",
    )(*ins)


def split_left(x):
    hi = x.astype(jnp.bfloat16)
    lo = (x - hi.astype(jnp.float32)).astype(jnp.bfloat16)
    return jnp.concatenate([hi, lo, hi], axis=1)


def split_right(x):
    hi = x.astype(jnp.bfloat16)
    lo = (x - hi.astype(jnp.float32)).astype(jnp.bfloat16)
    return jnp.concatenate([hi, hi, lo], axis=0)


def mul(a, b):
    return jnp.dot(split_left(a), split_right(b), preferred_element_type=jnp.float32)


def product_kernel(counts, tiled, n_done, blocks_ref, *refs):
    terms = []
    for n in counts:
        terms.append((refs[:n], refs[n]))
        refs = refs[n + 1 :]
    base_ref, done, outs = refs[0], refs[1 : 1 + n_done], refs[1 + n_done :]

    def flat(x):
        return x.reshape(x.shape[0] * x.shape[1], x.shape[2])

    def left(holders, j):
        x = holders[0][:, j]
        for ref in holders[1:]:
            x = x + ref[:, j]
        return flat(x)

    re, im = base_ref[0], base_ref[1]
    for holders, panel_ref in terms:
        s_re, s_im = left(holders, 0), left(holders, 1)
        g_re, g_im = flat(panel_ref[:, 0]), flat(panel_ref[:, 1])
        one = mul(s_re, g_re)
        two = mul(s_im, g_im)
        three = mul(s_re + s_im, g_re + g_im)
        re, im = re + (one - two), im + (three - one - two)
    rows = re.shape[0]
    for i, pair in enumerate([(ref[0], ref[1]) for ref in done] + [(re, im)]):
        for j in range(2):
            outs[0][j, i * rows : (i + 1) * rows] = pair[j]
            if tiled:
                slabs = outs[1].shape[0] // (n_done + 1)
                outs[1][i * slabs : (i + 1) * slabs, j] = pair[j].reshape(
                    (slabs,) + outs[1].shape[2:]
                )


def product(terms, panel, base, chunk=0, done=(), tiled=False):
    slabs, _, high, cols = terms[0][0][0].shape
    rows = slabs * high
    per = cols // panel.shape[2]
    full = lambda shape: pl.BlockSpec(shape, lambda i, b: (0,) * len(shape))
    in_specs, ins = [], []
    for j, (lefts, _) in enumerate(terms):
        in_specs += [full(x.shape) for x in lefts]
        in_specs.append(
            pl.BlockSpec((per,) + panel.shape[1:], lambda i, b, j=j: (b[j], 0, 0, 0))
        )
        ins += list(lefts) + [panel]
    at = chunk if base.shape[1] != rows else 0
    in_specs.append(pl.BlockSpec((2, rows, cols), lambda i, b: (0, at, 0)))
    in_specs += [full(x.shape) for x in done]
    outs = [jax.ShapeDtypeStruct((2, rows * (1 + len(done)), cols), jnp.float32)]
    if tiled:
        outs.append(jax.ShapeDtypeStruct((slabs * (1 + len(done)), 2, high, cols), jnp.float32))
    counts = [len(lefts) for lefts, _ in terms]
    return pl.pallas_call(
        lambda *refs: product_kernel(counts, tiled, len(done), *refs),
        out_shape=outs,
        grid_spec=pltpu.PrefetchScalarGridSpec(
            num_scalar_prefetch=1,
            grid=(1,),
            in_specs=in_specs,
            out_specs=[full(o.shape) for o in outs],
        ),
        compiler_params=pltpu.CompilerParams(vmem_limit_bytes=VMEM),
        name="product_last" if done else "product",
    )(jnp.stack([block for _, block in terms]), *ins, base, *done)


def time_product(sigma, panel, free, tiled):
    zl = lax.axis_index("zl")
    low = zl < 2
    near_block = lax.bitwise_xor(zl, 1)
    two_block, far_block = jnp.where(low, 2, 1), jnp.where(low, 3, 0)
    slabs = sigma.shape[0] // CHUNKS
    mine = [sigma[i * slabs : (i + 1) * slabs] for i in range(CHUNKS)]
    across, middle, outwards = [(0, 1), (1, 0), (2, 3), (3, 2)], [(1, 2), (2, 1)], [(1, 0), (2, 3)]

    def send(xs, pairs):
        out = []
        for x in xs:
            out.append(lax.ppermute(x, "zl", pairs))
        return out

    mid = send(mine, middle)
    near = send(mine, across)
    end_two = send(mid, outwards)
    mid_far = send(near, middle)
    end_far = send(mid_far, outwards)
    totals = []
    for i in range(CHUNKS):
        terms = [([mine[i]], zl), ([near[i]], near_block)]
        totals.append(product(terms, panel, free, i)[0])
    totals = [
        product([([mid[i], end_two[i]], two_block)], panel, totals[i])[0] for i in range(CHUNKS)
    ]
    done = []
    for i in range(CHUNKS):
        last = i == CHUNKS - 1
        res = product(
            [([mid_far[i], end_far[i]], far_block)],
            panel,
            totals[i],
            done=done if last else (),
            tiled=tiled and last,
        )
        done.append(res[0])
    return res


def pack(free, greater):
    return jnp.concatenate([free, greater], axis=0).swapaxes(0, 1)


def exchange(x):
    return lax.all_to_all(x, ("zh", "y"), 0, 0, tiled=True)


def body(g_free, g_greater_t, momentum_map, weights):
    momenta = momentum_map.shape[0]
    free, greater = g_free[:, 0], g_greater_t[:, 0]
    tile_rows, tile_cols = free.shape[1:]
    slabs = (2, momenta, tile_rows // momenta, tile_cols)
    weights = weights.reshape(-1, 1, tile_cols)

    green = free
    field = exchange(pack(free.reshape(slabs), greater.reshape(slabs)))
    mirror = None
    for sweep in range(ITERS):
        panel = lax.all_gather(green, ("x", "core"))
        panel = pltpu.with_memory_space_constraint(panel, pltpu.HBM)
        if mirror is None:
            sigma, mirror = self_energy(momentum_map, weights, field)
        else:
            sigma = self_energy(momentum_map, weights, field, mirror)
        sigma = exchange(sigma)
        if sweep == ITERS - 1:
            return time_product(sigma, panel, free, False)[0][:, None]
        green, tiles = time_product(sigma, panel, free, True)
        field = exchange(tiles)


def solution(mesh):
    fine = Mesh(mesh.devices.reshape(3, 8, 4, 4, 2), ("zh", "y", "zl", "x", "core"))
    spec = P(None, ("zh", "y"), ("x", "core"), "zl")
    return jax.shard_map(
        body, mesh=fine, in_specs=(spec, spec, P(), P()), out_specs=spec, check_vma=False
    )
```

profile of v0, /device:TPU:1, one launch (start us, length us, event | category | flops | bytes accessed | tf_op | source)
XLA Modules:
  0.0 270.2 jit_solution(13102097290531171372)
XLA Ops:
  7.3 2.4 copy_bitcast_fusion
  9.7 20.1 %all-to-all-start = ((f32[24,4,8,384]{3,2,1,0:T(8,128)}), f32[24,4,8,384]{3,2,1,0:T(8,128)S(1)}, u32[]{:S(2)}, u32[]{:S(2)}) async-start(f32[24,4,8,384]{3,2,1,0:T(8,128)} %copy_bitcast_fusion), calls=%async_computation | async-start | bytes 2359296 | tf_op jit(solution)/shard_map/all_to_all | solution.py:252
  29.9 40.9 %all-to-all-done.refs_2_ = f32[24,4,8,384]{3,2,1,0:T(8,128)S(1)} async-done(((f32[24,4,8,384]{3,2,1,0:T(8,128)}), f32[24,4,8,384]{3,2,1,0:T(8,128)S(1)}, u32[]{:S(2)}, u32[]{:S(2)}) %all-to-all-start) | async-done | bytes 1179680 | tf_op jit(solution)/shard_map/all_to_all | solution.py:252
  72.0 24.9 %all_to_all.20 = f32[24,2,8,384]{3,2,1,0:T(8,128)S(1)} all-to-all(f32[24,2,8,384]{3,2,1,0:T(8,128)S(1)} %get-tuple-element.9), channel_id=1, replica_groups=mesh['zh'=3,'y'=8,'zl'=4,'x'=4,'core'=2] {'zh','y'}, dimensions={0} | all-to-all | bytes 1179648 | tf_op jit(solution)/shard_map/all_to_all | solution.py:252
  96.9 1.9 collective-permute-start.5
  98.8 3.4 %collective-permute-start = (f32[12,2,8,384]{3,2,1,0:T(8,128)S(1)}, f32[12,2,8,384]{3,2,1,0:T(8,128)S(1)}, u32[]{:S(2)}, u32[]{:S(2)}) collective-permute-start(f32[12,2,8,384]{3,2,1,0:T(8,128)S(1)} %get-tuple-element.16.refs_1_), channel_id=1, source_target_pairs={{0,8},{8,0},{16,24},{24,16},{1,9},{9,1},{17,25},{25,17},{2,10},{10... | collective-permute-start | bytes 884744 | tf_op jit(solution)/shard_map/ppermute | solution.py:218
  103.5 3.3 %collective-permute-done.5.refs_3_ = f32[12,2,8,384]{3,2,1,0:T(8,128)S(1)} collective-permute-done((f32[12,2,8,384]{3,2,1,0:T(8,128)S(1)}, f32[12,2,8,384]{3,2,1,0:T(8,128)S(1)}, u32[]{:S(2)}, u32[]{:S(2)}) %collective-permute-start.5) | collective-permute-done | bytes 294944 | tf_op jit(solution)/shard_map/ppermute | solution.py:218
  107.5 5.6 %collective-permute-done.refs_3_ = f32[12,2,8,384]{3,2,1,0:T(8,128)S(1)} collective-permute-done((f32[12,2,8,384]{3,2,1,0:T(8,128)S(1)}, f32[12,2,8,384]{3,2,1,0:T(8,128)S(1)}, u32[]{:S(2)}, u32[]{:S(2)}) %collective-permute-start) | collective-permute-done | bytes 294944 | tf_op jit(solution)/shard_map/ppermute | solution.py:218
  119.1 3.2 %product.12.refs_4_ = f32[2,96,384]{2,1,0:T(8,128)S(1)} custom-call(s32[2]{0:T(128)S(1)} %pad_add_fusion.refs_0_, f32[12,2,8,384]{3,2,1,0:T(8,128)S(1)} %get-tuple-element.15.refs_1_, f32[8,2,192,384]{3,2,1,0:T(8,128)} %bitcast.27, f32[12,2,8,384]{3,2,1,0:T(8,128)S(1)} %collective-permute-done.5.refs_3_, f32[8,2,192,384]{3,2,1,0:T(8,128)} %bitcast.28, ...), custom_call_target="tpu_custom_call" | custom-call | tf_op jit(solution)/shard_map/product/pallas_call | solution.py:192
  122.4 3.2 %product.10.refs_4_ = f32[2,96,384]{2,1,0:T(8,128)S(1)} custom-call(s32[2]{0:T(128)S(1)} %pad_add_fusion.refs_0_, f32[12,2,8,384]{3,2,1,0:T(8,128)S(1)} %get-tuple-element.16.refs_1_, f32[8,2,192,384]{3,2,1,0:T(8,128)} %bitcast.29, f32[12,2,8,384]{3,2,1,0:T(8,128)S(1)} %collective-permute-done.refs_3_, f32[8,2,192,384]{3,2,1,0:T(8,128)} %bitcast.30, ...), custom_call_target="tpu_custom_call" | custom-call | tf_op jit(solution)/shard_map/product/pallas_call | solution.py:192
  125.6 7.3 %collective-permute-done.9.refs_2_ = f32[12,2,8,384]{3,2,1,0:T(8,128)} collective-permute-done((f32[12,2,8,384]{3,2,1,0:T(8,128)S(1)}, f32[12,2,8,384]{3,2,1,0:T(8,128)}, u32[]{:S(2)}, u32[]{:S(2)}) %collective-permute-start.9) | collective-permute-done | bytes 294944 | tf_op jit(solution)/shard_map/ppermute | solution.py:218
  133.0 2.0 product.13.refs_4_
  135.0 4.3 %collective-permute-done.4.refs_2_ = f32[12,2,8,384]{3,2,1,0:T(8,128)} collective-permute-done((f32[12,2,8,384]{3,2,1,0:T(8,128)S(1)}, f32[12,2,8,384]{3,2,1,0:T(8,128)}, u32[]{:S(2)}, u32[]{:S(2)}) %collective-permute-start.4) | collective-permute-done | bytes 294944 | tf_op jit(solution)/shard_map/ppermute | solution.py:218
  139.3 2.0 product.11.refs_4_
  141.3 4.3 %collective-permute-done.7.refs_2_ = f32[12,2,8,384]{3,2,1,0:T(8,128)} collective-permute-done((f32[12,2,8,384]{3,2,1,0:T(8,128)S(1)}, f32[12,2,8,384]{3,2,1,0:T(8,128)}, u32[]{:S(2)}, u32[]{:S(2)}) %collective-permute-start.7) | collective-permute-done | bytes 294944 | tf_op jit(solution)/shard_map/ppermute | solution.py:218
  145.6 2.0 product.14.refs_5_
  147.6 4.3 %collective-permute-done.2.refs_2_ = f32[12,2,8,384]{3,2,1,0:T(8,128)} collective-permute-done((f32[12,2,8,384]{3,2,1,0:T(8,128)S(1)}, f32[12,2,8,384]{3,2,1,0:T(8,128)}, u32[]{:S(2)}, u32[]{:S(2)}) %collective-permute-start.2) | collective-permute-done | bytes 294944 | tf_op jit(solution)/shard_map/ppermute | solution.py:218
  151.9 2.8 %product_last.2 = (f32[2,192,384]{2,1,0:T(8,128)}, f32[24,2,8,384]{3,2,1,0:T(8,128)S(1)}) custom-call(s32[1]{0:T(128)} %bitcast.refs_0_, f32[12,2,8,384]{3,2,1,0:T(8,128)S(1)} %collective-permute-done.1.refs_1_, f32[12,2,8,384]{3,2,1,0:T(8,128)} %collective-permute-done.2.refs_2_, f32[8,2,192,384]{3,2,1,0:T(8,128)} %bitcast.34, ...), custom_call_target="tpu_custom_call" | custom-call | tf_op jit(solution)/shard_map/product_last/pallas_call | solution.py:192
  154.8 24.6 %all_to_all.21.refs_2_ = f32[24,2,8,384]{3,2,1,0:T(8,128)S(1)} all-to-all(f32[24,2,8,384]{3,2,1,0:T(8,128)S(1)} %get-tuple-element.10), channel_id=1, replica_groups=mesh['zh'=3,'y'=8,'zl'=4,'x'=4,'core'=2] {'zh','y'}, dimensions={0} | all-to-all | bytes 1179648 | tf_op jit(solution)/shard_map/all_to_all | solution.py:252
  180.3 25.3 %all_to_all.22 = f32[24,2,8,384]{3,2,1,0:T(8,128)S(1)} all-to-all(f32[24,2,8,384]{3,2,1,0:T(8,128)S(1)} %self_energy_next.1), channel_id=1, replica_groups=mesh['zh'=3,'y'=8,'zl'=4,'x'=4,'core'=2] {'zh','y'}, dimensions={0} | all-to-all | bytes 1179648 | tf_op jit(solution)/shard_map/all_to_all | solution.py:252
  205.6 14.1 %collective-permute-start.15 = (f32[12,2,8,384]{3,2,1,0:T(8,128)S(1)}, f32[12,2,8,384]{3,2,1,0:T(8,128)S(1)}, u32[]{:S(2)}, u32[]{:S(2)}) collective-permute-start(f32[12,2,8,384]{3,2,1,0:T(8,128)S(1)} %get-tuple-element.13.refs_1_), channel_id=1, source_target_pairs={{0,8},{8,0},{16,24},{24,16},{1,9},{9,1},{17,25},{25,17},{2,10},{10... | collective-permute-start | bytes 884744 | tf_op jit(solution)/shard_map/ppermute | solution.py:218
  219.8 1.9 collective-permute-start.10
  222.4 3.9 %collective-permute-done.15.refs_3_ = f32[12,2,8,384]{3,2,1,0:T(8,128)S(1)} collective-permute-done((f32[12,2,8,384]{3,2,1,0:T(8,128)S(1)}, f32[12,2,8,384]{3,2,1,0:T(8,128)S(1)}, u32[]{:S(2)}, u32[]{:S(2)}) %collective-permute-start.15) | collective-permute-done | bytes 294944 | tf_op jit(solution)/shard_map/ppermute | solution.py:218
  227.7 5.0 %collective-permute-done.10.refs_3_ = f32[12,2,8,384]{3,2,1,0:T(8,128)S(1)} collective-permute-done((f32[12,2,8,384]{3,2,1,0:T(8,128)S(1)}, f32[12,2,8,384]{3,2,1,0:T(8,128)S(1)}, u32[]{:S(2)}, u32[]{:S(2)}) %collective-permute-start.10) | collective-permute-done | bytes 294944 | tf_op jit(solution)/shard_map/ppermute | solution.py:218
  238.8 3.2 %product.17.refs_4_ = f32[2,96,384]{2,1,0:T(8,128)S(1)} custom-call(s32[2]{0:T(128)S(1)} %pad_add_fusion.refs_0_, f32[12,2,8,384]{3,2,1,0:T(8,128)S(1)} %get-tuple-element.13.refs_1_, f32[8,2,192,384]{3,2,1,0:T(8,128)} %bitcast.19, f32[12,2,8,384]{3,2,1,0:T(8,128)S(1)} %collective-permute-done.15.refs_3_, f32[8,2,192,384]{3,2,1,0:T(8,128)} %bitcast.20, ...), custom_call_target="tpu_custom_call" | custom-call | tf_op jit(solution)/shard_map/product/pallas_call | solution.py:192
  242.0 3.2 %product.15.refs_4_ = f32[2,96,384]{2,1,0:T(8,128)S(1)} custom-call(s32[2]{0:T(128)S(1)} %pad_add_fusion.refs_0_, f32[12,2,8,384]{3,2,1,0:T(8,128)S(1)} %get-tuple-element.14.refs_1_, f32[8,2,192,384]{3,2,1,0:T(8,128)} %bitcast.21, f32[12,2,8,384]{3,2,1,0:T(8,128)S(1)} %collective-permute-done.10.refs_3_, f32[8,2,192,384]{3,2,1,0:T(8,128)} %bitcast.22, ...), custom_call_target="tpu_custom_call" | custom-call | tf_op jit(solution)/shard_map/product/pallas_call | solution.py:192
  245.3 2.0 product.18.refs_4_
  248.1 2.0 product.19.refs_5_
  250.1 4.3 %collective-permute-done.14.refs_2_ = f32[12,2,8,384]{3,2,1,0:T(8,128)S(1)} collective-permute-done((f32[12,2,8,384]{3,2,1,0:T(8,128)S(1)}, f32[12,2,8,384]{3,2,1,0:T(8,128)S(1)}, u32[]{:S(2)}, u32[]{:S(2)}) %collective-permute-start.14) | collective-permute-done | bytes 294944 | tf_op jit(solution)/shard_map/ppermute | solution.py:218
  254.5 1.9 product.16.refs_4_
  256.4 4.3 %collective-permute-done.12.refs_2_ = f32[12,2,8,384]{3,2,1,0:T(8,128)S(1)} collective-permute-done((f32[12,2,8,384]{3,2,1,0:T(8,128)S(1)}, f32[12,2,8,384]{3,2,1,0:T(8,128)S(1)}, u32[]{:S(2)}, u32[]{:S(2)}) %collective-permute-start.12) | collective-permute-done | bytes 294944 | tf_op jit(solution)/shard_map/ppermute | solution.py:218
  260.7 2.7 %product_last.3 = f32[2,192,384]{2,1,0:T(8,128)} custom-call(s32[1]{0:T(128)} %bitcast.refs_0_, f32[12,2,8,384]{3,2,1,0:T(8,128)S(1)} %collective-permute-done.11.refs_1_, f32[12,2,8,384]{3,2,1,0:T(8,128)S(1)} %collective-permute-done.12.refs_2_, f32[8,2,192,384]{3,2,1,0:T(8,128)} %bitcast.26, f32[2,96,384]{2,1,0:T(8,128)S(1)} %product.16.refs_4_, ...), custom_call_target="tpu_custom_call" | custom-call | tf_op jit(solution)/shard_map/product_last/pallas_call | solution.py:192
  (44 shorter events, 19.8 us)
Async XLA Ops:
  6.5 112.6 %all-gather.5.cloned.1.call-start = ((), (), s32[]{:S(2)}) async-start(), calls=%async_computation.4 | async-start | bytes 5308416 | tf_op jit(solution)/shard_map/all_gather | solution.py:266
  9.7 20.2 %copy-start.2 = (f32[1536]{0:T(1024)S(1)}, f32[1536]{0:T(1024)}, u32[]{:S(2)}) copy-start(f32[1536]{0:T(1024)} %param.7) | copy-start | bytes 18436
  9.7 61.1 %copy-start.1 = (s32[24]{0:T(128)S(1)}, s32[24]{0:T(128)}, u32[]{:S(2)}) copy-start(s32[24]{0:T(128)} %refs_0_.3) | copy-start | bytes 292
  9.7 61.1 %all-to-all-start = ((f32[24,4,8,384]{3,2,1,0:T(8,128)}), f32[24,4,8,384]{3,2,1,0:T(8,128)S(1)}, u32[]{:S(2)}, u32[]{:S(2)}) async-start(f32[24,4,8,384]{3,2,1,0:T(8,128)} %copy_bitcast_fusion), calls=%async_computation | async-start | bytes 2359296 | tf_op jit(solution)/shard_map/all_to_all | solution.py:252
  29.8 209.0 %all-gather.7.cloned.1.call-start = ((), (), s32[]{:S(2)}) async-start(), calls=%async_computation.5 | async-start | bytes 5308416 | tf_op jit(solution)/shard_map/all_gather | solution.py:266
  71.9 47.2 %copy-start = (f32[2,1,192,384]{3,2,1,0:T(8,128)S(1)}, f32[2,1,192,384]{3,2,1,0:T(8,128)}, u32[]{:S(2)}) copy-start(f32[2,1,192,384]{3,2,1,0:T(8,128)} %param.4) | copy-start | bytes 1769476
  96.9 9.9 %collective-permute-start.5 = (f32[12,2,8,384]{3,2,1,0:T(8,128)S(1)}, f32[12,2,8,384]{3,2,1,0:T(8,128)S(1)}, u32[]{:S(2)}, u32[]{:S(2)}) collective-permute-start(f32[12,2,8,384]{3,2,1,0:T(8,128)S(1)} %get-tuple-element.15.refs_1_), channel_id=1, source_target_pairs={{0,8},{8,0},{16,24},{24,16},{1,9},{9,1},{17,25},{25,17},{2,10},{10... | collective-permute-start | bytes 884744 | tf_op jit(solution)/shard_map/ppermute | solution.py:218
  98.8 14.3 %collective-permute-start = (f32[12,2,8,384]{3,2,1,0:T(8,128)S(1)}, f32[12,2,8,384]{3,2,1,0:T(8,128)S(1)}, u32[]{:S(2)}, u32[]{:S(2)}) collective-permute-start(f32[12,2,8,384]{3,2,1,0:T(8,128)S(1)} %get-tuple-element.16.refs_1_), channel_id=1, source_target_pairs={{0,8},{8,0},{16,24},{24,16},{1,9},{9,1},{17,25},{25,17},{2,10},{10... | collective-permute-start | bytes 884744 | tf_op jit(solution)/shard_map/ppermute | solution.py:218
  102.2 11.6 %collective-permute-start.8 = (f32[12,2,8,384]{3,2,1,0:T(8,128)S(1)}, f32[12,2,8,384]{3,2,1,0:T(8,128)S(1)}, u32[]{:S(2)}, u32[]{:S(2)}) collective-permute-start(f32[12,2,8,384]{3,2,1,0:T(8,128)S(1)} %get-tuple-element.15.refs_1_), channel_id=1, source_target_pairs={{8,16},{16,8},{9,17},{17,9},{10,18},{18,10},{11,19},{19,11},{12,20... | collective-permute-start | bytes 884744 | tf_op jit(solution)/shard_map/ppermute | solution.py:218
  102.9 12.2 %collective-permute-start.3 = (f32[12,2,8,384]{3,2,1,0:T(8,128)S(1)}, f32[12,2,8,384]{3,2,1,0:T(8,128)S(1)}, u32[]{:S(2)}, u32[]{:S(2)}) collective-permute-start(f32[12,2,8,384]{3,2,1,0:T(8,128)S(1)} %get-tuple-element.16.refs_1_), channel_id=1, source_target_pairs={{8,16},{16,8},{9,17},{17,9},{10,18},{18,10},{11,19},{19,11},{12,20... | collective-permute-start | bytes 884744 | tf_op jit(solution)/shard_map/ppermute | solution.py:218
  106.8 9.6 %collective-permute-start.6 = (f32[12,2,8,384]{3,2,1,0:T(8,128)S(1)}, f32[12,2,8,384]{3,2,1,0:T(8,128)S(1)}, u32[]{:S(2)}, u32[]{:S(2)}) collective-permute-start(f32[12,2,8,384]{3,2,1,0:T(8,128)S(1)} %collective-permute-done.5.refs_3_), channel_id=1, source_target_pairs={{8,16},{16,8},{9,17},{17,9},{10,18},{18,10},{11,19},{19,11},{12,20... | collective-permute-start | bytes 884744 | tf_op jit(solution)/shard_map/ppermute | solution.py:218
  113.1 4.6 %collective-permute-start.1 = (f32[12,2,8,384]{3,2,1,0:T(8,128)S(1)}, f32[12,2,8,384]{3,2,1,0:T(8,128)S(1)}, u32[]{:S(2)}, u32[]{:S(2)}) collective-permute-start(f32[12,2,8,384]{3,2,1,0:T(8,128)S(1)} %collective-permute-done.refs_3_), channel_id=1, source_target_pairs={{8,16},{16,8},{9,17},{17,9},{10,18},{18,10},{11,19},{19,11},{12,20... | collective-permute-start | bytes 884744 | tf_op jit(solution)/shard_map/ppermute | solution.py:218
  113.8 19.2 %collective-permute-start.9 = (f32[12,2,8,384]{3,2,1,0:T(8,128)S(1)}, f32[12,2,8,384]{3,2,1,0:T(8,128)}, u32[]{:S(2)}, u32[]{:S(2)}) collective-permute-start(f32[12,2,8,384]{3,2,1,0:T(8,128)S(1)} %collective-permute-done.8.refs_1_), channel_id=1, source_target_pairs={{8,0},{16,24},{9,1},{17,25},{10,2},{18,26},{11,3},{19,27},{12,4},{... | collective-permute-start | bytes 884744 | tf_op jit(solution)/shard_map/ppermute | solution.py:218
  115.1 24.2 %collective-permute-start.4 = (f32[12,2,8,384]{3,2,1,0:T(8,128)S(1)}, f32[12,2,8,384]{3,2,1,0:T(8,128)}, u32[]{:S(2)}, u32[]{:S(2)}) collective-permute-start(f32[12,2,8,384]{3,2,1,0:T(8,128)S(1)} %collective-permute-done.3.refs_1_), channel_id=1, source_target_pairs={{8,0},{16,24},{9,1},{17,25},{10,2},{18,26},{11,3},{19,27},{12,4},{... | collective-permute-start | bytes 884744 | tf_op jit(solution)/shard_map/ppermute | solution.py:218
  116.4 29.2 %collective-permute-start.7 = (f32[12,2,8,384]{3,2,1,0:T(8,128)S(1)}, f32[12,2,8,384]{3,2,1,0:T(8,128)}, u32[]{:S(2)}, u32[]{:S(2)}) collective-permute-start(f32[12,2,8,384]{3,2,1,0:T(8,128)S(1)} %collective-permute-done.6.refs_1_), channel_id=1, source_target_pairs={{8,0},{16,24},{9,1},{17,25},{10,2},{18,26},{11,3},{19,27},{12,4},{... | collective-permute-start | bytes 884744 | tf_op jit(solution)/shard_map/ppermute | solution.py:218
  117.7 34.2 %collective-permute-start.2 = (f32[12,2,8,384]{3,2,1,0:T(8,128)S(1)}, f32[12,2,8,384]{3,2,1,0:T(8,128)}, u32[]{:S(2)}, u32[]{:S(2)}) collective-permute-start(f32[12,2,8,384]{3,2,1,0:T(8,128)S(1)} %collective-permute-done.1.refs_1_), channel_id=1, source_target_pairs={{8,0},{16,24},{9,1},{17,25},{10,2},{18,26},{11,3},{19,27},{12,4},{... | collective-permute-start | bytes 884744 | tf_op jit(solution)/shard_map/ppermute | solution.py:218
  205.6 20.7 %collective-permute-start.15 = (f32[12,2,8,384]{3,2,1,0:T(8,128)S(1)}, f32[12,2,8,384]{3,2,1,0:T(8,128)S(1)}, u32[]{:S(2)}, u32[]{:S(2)}) collective-permute-start(f32[12,2,8,384]{3,2,1,0:T(8,128)S(1)} %get-tuple-element.13.refs_1_), channel_id=1, source_target_pairs={{0,8},{8,0},{16,24},{24,16},{1,9},{9,1},{17,25},{25,17},{2,10},{10... | collective-permute-start | bytes 884744 | tf_op jit(solution)/shard_map/ppermute | solution.py:218
  219.8 12.9 %collective-permute-start.10 = (f32[12,2,8,384]{3,2,1,0:T(8,128)S(1)}, f32[12,2,8,384]{3,2,1,0:T(8,128)S(1)}, u32[]{:S(2)}, u32[]{:S(2)}) collective-permute-start(f32[12,2,8,384]{3,2,1,0:T(8,128)S(1)} %get-tuple-element.14.refs_1_), channel_id=1, source_target_pairs={{0,8},{8,0},{16,24},{24,16},{1,9},{9,1},{17,25},{25,17},{2,10},{10... | collective-permute-start | bytes 884744 | tf_op jit(solution)/shard_map/ppermute | solution.py:218
  221.7 11.6 %collective-permute-start.18 = (f32[12,2,8,384]{3,2,1,0:T(8,128)S(1)}, f32[12,2,8,384]{3,2,1,0:T(8,128)S(1)}, u32[]{:S(2)}, u32[]{:S(2)}) collective-permute-start(f32[12,2,8,384]{3,2,1,0:T(8,128)S(1)} %get-tuple-element.13.refs_1_), channel_id=1, source_target_pairs={{8,16},{16,8},{9,17},{17,9},{10,18},{18,10},{11,19},{19,11},{12,20... | collective-permute-start | bytes 884744 | tf_op jit(solution)/shard_map/ppermute | solution.py:218
  226.3 8.3 %collective-permute-start.16 = (f32[12,2,8,384]{3,2,1,0:T(8,128)S(1)}, f32[12,2,8,384]{3,2,1,0:T(8,128)S(1)}, u32[]{:S(2)}, u32[]{:S(2)}) collective-permute-start(f32[12,2,8,384]{3,2,1,0:T(8,128)S(1)} %collective-permute-done.15.refs_3_), channel_id=1, source_target_pairs={{8,16},{16,8},{9,17},{17,9},{10,18},{18,10},{11,19},{19,11},{12,20... | collective-permute-start | bytes 884744 | tf_op jit(solution)/shard_map/ppermute | solution.py:218
  227.0 8.9 %collective-permute-start.13 = (f32[12,2,8,384]{3,2,1,0:T(8,128)S(1)}, f32[12,2,8,384]{3,2,1,0:T(8,128)S(1)}, u32[]{:S(2)}, u32[]{:S(2)}) collective-permute-start(f32[12,2,8,384]{3,2,1,0:T(8,128)S(1)} %get-tuple-element.14.refs_1_), channel_id=1, source_target_pairs={{8,16},{16,8},{9,17},{17,9},{10,18},{18,10},{11,19},{19,11},{12,20... | collective-permute-start | bytes 884744 | tf_op jit(solution)/shard_map/ppermute | solution.py:218
  232.6 4.6 %collective-permute-start.11 = (f32[12,2,8,384]{3,2,1,0:T(8,128)S(1)}, f32[12,2,8,384]{3,2,1,0:T(8,128)S(1)}, u32[]{:S(2)}, u32[]{:S(2)}) collective-permute-start(f32[12,2,8,384]{3,2,1,0:T(8,128)S(1)} %collective-permute-done.10.refs_3_), channel_id=1, source_target_pairs={{8,16},{16,8},{9,17},{17,9},{10,18},{18,10},{11,19},{19,11},{12,20... | collective-permute-start | bytes 884744 | tf_op jit(solution)/shard_map/ppermute | solution.py:218
  233.3 12.0 %collective-permute-start.19 = (f32[12,2,8,384]{3,2,1,0:T(8,128)S(1)}, f32[12,2,8,384]{3,2,1,0:T(8,128)}, u32[]{:S(2)}, u32[]{:S(2)}) collective-permute-start(f32[12,2,8,384]{3,2,1,0:T(8,128)S(1)} %collective-permute-done.18.refs_1_), channel_id=1, source_target_pairs={{8,0},{16,24},{9,1},{17,25},{10,2},{18,26},{11,3},{19,27},{12,4},{... | collective-permute-start | bytes 884744 | tf_op jit(solution)/shard_map/ppermute | solution.py:218
  234.6 13.5 %collective-permute-start.17 = (f32[12,2,8,384]{3,2,1,0:T(8,128)S(1)}, f32[12,2,8,384]{3,2,1,0:T(8,128)}, u32[]{:S(2)}, u32[]{:S(2)}) collective-permute-start(f32[12,2,8,384]{3,2,1,0:T(8,128)S(1)} %collective-permute-done.16.refs_1_), channel_id=1, source_target_pairs={{8,0},{16,24},{9,1},{17,25},{10,2},{18,26},{11,3},{19,27},{12,4},{... | collective-permute-start | bytes 884744 | tf_op jit(solution)/shard_map/ppermute | solution.py:218
  235.9 18.5 %collective-permute-start.14 = (f32[12,2,8,384]{3,2,1,0:T(8,128)S(1)}, f32[12,2,8,384]{3,2,1,0:T(8,128)S(1)}, u32[]{:S(2)}, u32[]{:S(2)}) collective-permute-start(f32[12,2,8,384]{3,2,1,0:T(8,128)S(1)} %collective-permute-done.13.refs_1_), channel_id=1, source_target_pairs={{8,0},{16,24},{9,1},{17,25},{10,2},{18,26},{11,3},{19,27},{12,4},{... | collective-permute-start | bytes 884744 | tf_op jit(solution)/shard_map/ppermute | solution.py:218
  237.3 23.4 %collective-permute-start.12 = (f32[12,2,8,384]{3,2,1,0:T(8,128)S(1)}, f32[12,2,8,384]{3,2,1,0:T(8,128)S(1)}, u32[]{:S(2)}, u32[]{:S(2)}) collective-permute-start(f32[12,2,8,384]{3,2,1,0:T(8,128)S(1)} %collective-permute-done.11.refs_1_), channel_id=1, source_target_pairs={{8,0},{16,24},{9,1},{17,25},{10,2},{18,26},{11,3},{19,27},{12,4},{... | collective-permute-start | bytes 884744 | tf_op jit(solution)/shard_map/ppermute | solution.py:218
Sparse Core Ops, SparseCore 0:
  9.7 50.2 all-gather.4
  154.9 39.9 all-gather.6
where the time goes:
time: 275 us; the launch traced here: 270 us
  waiting for transfers between devices  89.2 us (32%)
  blocking collectives  74.7 us (27%)
  starting transfers between devices  57.4 us (21%)
  Pallas kernels  32.6 us (12%)
  between operations  13.8 us (5%)
    all_to_all x3, blocking collectives, exchange(): return lax.all_to_all(x, ('zh', 'y'), 0, 0, tiled=True)  74.7 us
    ppermute x20, waiting for transfers between devices, send(): out.append(lax.ppermute(x, 'zl', pairs))  47.5 us
    all_to_all x1, waiting for transfers between devices, exchange(): return lax.all_to_all(x, ('zh', 'y'), 0, 0, tiled=True)  40.9 us
    ppermute x20, starting transfers between devices, send(): out.append(lax.ppermute(x, 'zl', pairs))  37.2 us
    pallas_call x12, Pallas kernels, product(): pl.pallas_call(lambda *refs: product_kernel(counts, tiled, len(done), *re...  30.5 us
    all_to_all x1, starting transfers between devices, exchange(): return lax.all_to_all(x, ('zh', 'y'), 0, 0, tiled=True)  20.1 us
  transfers between devices with their start and end apart: 23, of which 12 were waited for; matrix products, arithmetic and copies ran while one was open for 1% of the time, Pallas kernels for 10%

commit v1 on v0

--- a/solution.py
+++ b/solution.py
@@ -12,7 +12,7 @@
 
 
 CHUNKS = 2
-VMEM = 24 * 1024 * 1024
+VMEM = 16 * 1024 * 1024
 
 LANES = 128
 ROOT3_2 = math.sqrt(3.0) / 2.0
@@ -70,8 +70,9 @@
     else:
         mirror_ref, sigma_ref, where_ref = refs
     momenta = field_ref.shape[0]
+    ny, nz = lax.axis_size("y"), lax.axis_size("zh")
     for k in range(momenta):
-        where_ref[map_ref[k]] = k
+        where_ref[map_ref[k]] = k % ny * nz + k // ny
     spot = [where_ref[q] for q in range(momenta)]
     zl = lax.axis_index("zl")
     for lane in range(0, field_ref.shape[3], LANES):
@@ -249,7 +250,7 @@
 
 
 def exchange(x):
-    return lax.all_to_all(x, ("zh", "y"), 0, 0, tiled=True)
+    return lax.all_to_all(x, ("y", "zh"), 0, 0, tiled=True)
 
 
 def body(g_free, g_greater_t, momentum_map, weights):

time: 275 us -> 275 us (level)
  waiting for transfers between devices: 89.2 us -> 96.7 us
  blocking collectives: 74.7 us -> 69.7 us
  starting transfers between devices: 57.4 us -> 54.5 us
    ppermute x20, waiting for transfers between devices: 47.5 us -> 56.9 us  [send(): out.append(lax.ppermute(x, 'zl', pairs))]
    all_to_all x3, blocking collectives: 74.7 us -> 69.7 us  [exchange(): return lax.all_to_all(x, ('y', 'zh'), 0, 0, tiled=True)]
    ppermute x20, starting transfers between devices: 37.2 us -> 34.4 us  [send(): out.append(lax.ppermute(x, 'zl', pairs))]
where the time goes in v1:
time: 275 us; the launch traced here: 270 us
  waiting for transfers between devices  96.7 us (35%)
  blocking collectives  69.7 us (25%)
  starting transfers between devices  54.5 us (20%)
  Pallas kernels  32.6 us (12%)
  between operations  13.8 us (5%)
    all_to_all x3, blocking collectives, exchange(): return lax.all_to_all(x, ('y', 'zh'), 0, 0, tiled=True)  69.7 us
    ppermute x20, waiting for transfers between devices, send(): out.append(lax.ppermute(x, 'zl', pairs))  56.9 us
    all_to_all x1, waiting for transfers between devices, exchange(): return lax.all_to_all(x, ('y', 'zh'), 0, 0, tiled=True)  39.1 us
    ppermute x20, starting transfers between devices, send(): out.append(lax.ppermute(x, 'zl', pairs))  34.4 us
    pallas_call x12, Pallas kernels, product(): pl.pallas_call(lambda *refs: product_kernel(counts, tiled, len(done), *re...  30.5 us
    all_to_all x1, starting transfers between devices, exchange(): return lax.all_to_all(x, ('y', 'zh'), 0, 0, tiled=True)  20.1 us
  transfers between devices with their start and end apart: 23, of which 12 were waited for; matrix products, arithmetic and copies ran while one was open for 1% of the time, Pallas kernels for 10%

profile of v1, /device:TPU:1, one launch (start us, length us, event | category | flops | bytes accessed | tf_op | source)
XLA Modules:
  0.0 269.9 jit_solution(17907119772512362540)
XLA Ops:
  7.3 2.4 copy_bitcast_fusion
  9.7 20.1 %all-to-all-start = ((f32[24,4,8,384]{3,2,1,0:T(8,128)}), f32[24,4,8,384]{3,2,1,0:T(8,128)S(1)}, u32[]{:S(2)}, u32[]{:S(2)}) async-start(f32[24,4,8,384]{3,2,1,0:T(8,128)} %copy_bitcast_fusion), calls=%async_computation | async-start | bytes 2359296 | tf_op jit(solution)/shard_map/all_to_all | solution.py:253
  29.9 39.1 %all-to-all-done.refs_2_ = f32[24,4,8,384]{3,2,1,0:T(8,128)S(1)} async-done(((f32[24,4,8,384]{3,2,1,0:T(8,128)}), f32[24,4,8,384]{3,2,1,0:T(8,128)S(1)}, u32[]{:S(2)}, u32[]{:S(2)}) %all-to-all-start) | async-done | bytes 1179680 | tf_op jit(solution)/shard_map/all_to_all | solution.py:253
  70.1 22.1 %all_to_all.20 = f32[24,2,8,384]{3,2,1,0:T(8,128)S(1)} all-to-all(f32[24,2,8,384]{3,2,1,0:T(8,128)S(1)} %get-tuple-element.9), channel_id=1, replica_groups=mesh['zh'=3,'y'=8,'zl'=4,'x'=4,'core'=2] {'y','zh'}, dimensions={0} | all-to-all | bytes 1179648 | tf_op jit(solution)/shard_map/all_to_all | solution.py:253
  92.3 1.9 collective-permute-start.5
  94.2 3.4 %collective-permute-start = (f32[12,2,8,384]{3,2,1,0:T(8,128)S(1)}, f32[12,2,8,384]{3,2,1,0:T(8,128)S(1)}, u32[]{:S(2)}, u32[]{:S(2)}) collective-permute-start(f32[12,2,8,384]{3,2,1,0:T(8,128)S(1)} %get-tuple-element.16.refs_1_), channel_id=1, source_target_pairs={{0,8},{8,0},{16,24},{24,16},{1,9},{9,1},{17,25},{25,17},{2,10},{10... | collective-permute-start | bytes 884744 | tf_op jit(solution)/shard_map/ppermute | solution.py:219
  98.9 3.0 %collective-permute-done.5.refs_3_ = f32[12,2,8,384]{3,2,1,0:T(8,128)S(1)} collective-permute-done((f32[12,2,8,384]{3,2,1,0:T(8,128)S(1)}, f32[12,2,8,384]{3,2,1,0:T(8,128)S(1)}, u32[]{:S(2)}, u32[]{:S(2)}) %collective-permute-start.5) | collective-permute-done | bytes 294944 | tf_op jit(solution)/shard_map/ppermute | solution.py:219
  102.6 5.6 %collective-permute-done.refs_3_ = f32[12,2,8,384]{3,2,1,0:T(8,128)S(1)} collective-permute-done((f32[12,2,8,384]{3,2,1,0:T(8,128)S(1)}, f32[12,2,8,384]{3,2,1,0:T(8,128)S(1)}, u32[]{:S(2)}, u32[]{:S(2)}) %collective-permute-start) | collective-permute-done | bytes 294944 | tf_op jit(solution)/shard_map/ppermute | solution.py:219
  114.3 3.2 %product.12.refs_4_ = f32[2,96,384]{2,1,0:T(8,128)S(1)} custom-call(s32[2]{0:T(128)S(1)} %pad_add_fusion.refs_0_, f32[12,2,8,384]{3,2,1,0:T(8,128)S(1)} %get-tuple-element.15.refs_1_, f32[8,2,192,384]{3,2,1,0:T(8,128)} %bitcast.27, f32[12,2,8,384]{3,2,1,0:T(8,128)S(1)} %collective-permute-done.5.refs_3_, f32[8,2,192,384]{3,2,1,0:T(8,128)} %bitcast.28, ...), custom_call_target="tpu_custom_call" | custom-call | tf_op jit(solution)/shard_map/product/pallas_call | solution.py:193
  117.5 3.2 %product.10.refs_4_ = f32[2,96,384]{2,1,0:T(8,128)S(1)} custom-call(s32[2]{0:T(128)S(1)} %pad_add_fusion.refs_0_, f32[12,2,8,384]{3,2,1,0:T(8,128)S(1)} %get-tuple-element.16.refs_1_, f32[8,2,192,384]{3,2,1,0:T(8,128)} %bitcast.29, f32[12,2,8,384]{3,2,1,0:T(8,128)S(1)} %collective-permute-done.refs_3_, f32[8,2,192,384]{3,2,1,0:T(8,128)} %bitcast.30, ...), custom_call_target="tpu_custom_call" | custom-call | tf_op jit(solution)/shard_map/product/pallas_call | solution.py:193
  120.8 16.8 %collective-permute-done.9.refs_2_ = f32[12,2,8,384]{3,2,1,0:T(8,128)} collective-permute-done((f32[12,2,8,384]{3,2,1,0:T(8,128)S(1)}, f32[12,2,8,384]{3,2,1,0:T(8,128)}, u32[]{:S(2)}, u32[]{:S(2)}) %collective-permute-start.9) | collective-permute-done | bytes 294944 | tf_op jit(solution)/shard_map/ppermute | solution.py:219
  137.5 2.0 product.13.refs_4_
  139.6 4.3 %collective-permute-done.4.refs_2_ = f32[12,2,8,384]{3,2,1,0:T(8,128)} collective-permute-done((f32[12,2,8,384]{3,2,1,0:T(8,128)S(1)}, f32[12,2,8,384]{3,2,1,0:T(8,128)}, u32[]{:S(2)}, u32[]{:S(2)}) %collective-permute-start.4) | collective-permute-done | bytes 294944 | tf_op jit(solution)/shard_map/ppermute | solution.py:219
  143.9 2.0 product.11.refs_4_
  145.9 4.3 %collective-permute-done.7.refs_2_ = f32[12,2,8,384]{3,2,1,0:T(8,128)} collective-permute-done((f32[12,2,8,384]{3,2,1,0:T(8,128)S(1)}, f32[12,2,8,384]{3,2,1,0:T(8,128)}, u32[]{:S(2)}, u32[]{:S(2)}) %collective-permute-start.7) | collective-permute-done | bytes 294944 | tf_op jit(solution)/shard_map/ppermute | solution.py:219
  150.2 2.0 product.14.refs_5_
  152.2 4.3 %collective-permute-done.2.refs_2_ = f32[12,2,8,384]{3,2,1,0:T(8,128)} collective-permute-done((f32[12,2,8,384]{3,2,1,0:T(8,128)S(1)}, f32[12,2,8,384]{3,2,1,0:T(8,128)}, u32[]{:S(2)}, u32[]{:S(2)}) %collective-permute-start.2) | collective-permute-done | bytes 294944 | tf_op jit(solution)/shard_map/ppermute | solution.py:219
  156.5 2.8 %product_last.2 = (f32[2,192,384]{2,1,0:T(8,128)}, f32[24,2,8,384]{3,2,1,0:T(8,128)S(1)}) custom-call(s32[1]{0:T(128)} %bitcast.refs_0_, f32[12,2,8,384]{3,2,1,0:T(8,128)S(1)} %collective-permute-done.1.refs_1_, f32[12,2,8,384]{3,2,1,0:T(8,128)} %collective-permute-done.2.refs_2_, f32[8,2,192,384]{3,2,1,0:T(8,128)} %bitcast.34, ...), custom_call_target="tpu_custom_call" | custom-call | tf_op jit(solution)/shard_map/product_last/pallas_call | solution.py:193
  159.4 22.8 %all_to_all.21.refs_2_ = f32[24,2,8,384]{3,2,1,0:T(8,128)S(1)} all-to-all(f32[24,2,8,384]{3,2,1,0:T(8,128)S(1)} %get-tuple-element.10), channel_id=1, replica_groups=mesh['zh'=3,'y'=8,'zl'=4,'x'=4,'core'=2] {'y','zh'}, dimensions={0} | all-to-all | bytes 1179648 | tf_op jit(solution)/shard_map/all_to_all | solution.py:253
  183.1 24.8 %all_to_all.22 = f32[24,2,8,384]{3,2,1,0:T(8,128)S(1)} all-to-all(f32[24,2,8,384]{3,2,1,0:T(8,128)S(1)} %self_energy_next.1), channel_id=1, replica_groups=mesh['zh'=3,'y'=8,'zl'=4,'x'=4,'core'=2] {'y','zh'}, dimensions={0} | all-to-all | bytes 1179648 | tf_op jit(solution)/shard_map/all_to_all | solution.py:253
  208.0 11.3 %collective-permute-start.15 = (f32[12,2,8,384]{3,2,1,0:T(8,128)S(1)}, f32[12,2,8,384]{3,2,1,0:T(8,128)S(1)}, u32[]{:S(2)}, u32[]{:S(2)}) collective-permute-start(f32[12,2,8,384]{3,2,1,0:T(8,128)S(1)} %get-tuple-element.13.refs_1_), channel_id=1, source_target_pairs={{0,8},{8,0},{16,24},{24,16},{1,9},{9,1},{17,25},{25,17},{2,10},{10... | collective-permute-start | bytes 884744 | tf_op jit(solution)/shard_map/ppermute | solution.py:219
  219.2 1.9 collective-permute-start.10
  221.9 3.9 %collective-permute-done.15.refs_3_ = f32[12,2,8,384]{3,2,1,0:T(8,128)S(1)} collective-permute-done((f32[12,2,8,384]{3,2,1,0:T(8,128)S(1)}, f32[12,2,8,384]{3,2,1,0:T(8,128)S(1)}, u32[]{:S(2)}, u32[]{:S(2)}) %collective-permute-start.15) | collective-permute-done | bytes 294944 | tf_op jit(solution)/shard_map/ppermute | solution.py:219
  227.1 5.0 %collective-permute-done.10.refs_3_ = f32[12,2,8,384]{3,2,1,0:T(8,128)S(1)} collective-permute-done((f32[12,2,8,384]{3,2,1,0:T(8,128)S(1)}, f32[12,2,8,384]{3,2,1,0:T(8,128)S(1)}, u32[]{:S(2)}, u32[]{:S(2)}) %collective-permute-start.10) | collective-permute-done | bytes 294944 | tf_op jit(solution)/shard_map/ppermute | solution.py:219
  238.2 3.2 %product.17.refs_4_ = f32[2,96,384]{2,1,0:T(8,128)S(1)} custom-call(s32[2]{0:T(128)S(1)} %pad_add_fusion.refs_0_, f32[12,2,8,384]{3,2,1,0:T(8,128)S(1)} %get-tuple-element.13.refs_1_, f32[8,2,192,384]{3,2,1,0:T(8,128)} %bitcast.19, f32[12,2,8,384]{3,2,1,0:T(8,128)S(1)} %collective-permute-done.15.refs_3_, f32[8,2,192,384]{3,2,1,0:T(8,128)} %bitcast.20, ...), custom_call_target="tpu_custom_call" | custom-call | tf_op jit(solution)/shard_map/product/pallas_call | solution.py:193
  241.5 3.2 %product.15.refs_4_ = f32[2,96,384]{2,1,0:T(8,128)S(1)} custom-call(s32[2]{0:T(128)S(1)} %pad_add_fusion.refs_0_, f32[12,2,8,384]{3,2,1,0:T(8,128)S(1)} %get-tuple-element.14.refs_1_, f32[8,2,192,384]{3,2,1,0:T(8,128)} %bitcast.21, f32[12,2,8,384]{3,2,1,0:T(8,128)S(1)} %collective-permute-done.10.refs_3_, f32[8,2,192,384]{3,2,1,0:T(8,128)} %bitcast.22, ...), custom_call_target="tpu_custom_call" | custom-call | tf_op jit(solution)/shard_map/product/pallas_call | solution.py:193
  244.7 2.0 product.18.refs_4_
  247.8 2.0 product.19.refs_5_
  249.8 4.3 %collective-permute-done.14.refs_2_ = f32[12,2,8,384]{3,2,1,0:T(8,128)S(1)} collective-permute-done((f32[12,2,8,384]{3,2,1,0:T(8,128)S(1)}, f32[12,2,8,384]{3,2,1,0:T(8,128)S(1)}, u32[]{:S(2)}, u32[]{:S(2)}) %collective-permute-start.14) | collective-permute-done | bytes 294944 | tf_op jit(solution)/shard_map/ppermute | solution.py:219
  254.1 1.9 product.16.refs_4_
  256.0 4.3 %collective-permute-done.12.refs_2_ = f32[12,2,8,384]{3,2,1,0:T(8,128)S(1)} collective-permute-done((f32[12,2,8,384]{3,2,1,0:T(8,128)S(1)}, f32[12,2,8,384]{3,2,1,0:T(8,128)S(1)}, u32[]{:S(2)}, u32[]{:S(2)}) %collective-permute-start.12) | collective-permute-done | bytes 294944 | tf_op jit(solution)/shard_map/ppermute | solution.py:219
  260.3 2.7 %product_last.3 = f32[2,192,384]{2,1,0:T(8,128)} custom-call(s32[1]{0:T(128)} %bitcast.refs_0_, f32[12,2,8,384]{3,2,1,0:T(8,128)S(1)} %collective-permute-done.11.refs_1_, f32[12,2,8,384]{3,2,1,0:T(8,128)S(1)} %collective-permute-done.12.refs_2_, f32[8,2,192,384]{3,2,1,0:T(8,128)} %bitcast.26, f32[2,96,384]{2,1,0:T(8,128)S(1)} %product.16.refs_4_, ...), custom_call_target="tpu_custom_call" | custom-call | tf_op jit(solution)/shard_map/product_last/pallas_call | solution.py:193
  (44 shorter events, 20.0 us)
Async XLA Ops:
  6.5 107.7 %all-gather.5.cloned.1.call-start = ((), (), s32[]{:S(2)}) async-start(), calls=%async_computation.4 | async-start | bytes 5308416 | tf_op jit(solution)/shard_map/all_gather | solution.py:267
  9.7 20.2 %copy-start.2 = (f32[1536]{0:T(1024)S(1)}, f32[1536]{0:T(1024)}, u32[]{:S(2)}) copy-start(f32[1536]{0:T(1024)} %param.7) | copy-start | bytes 18436
  9.7 59.3 %copy-start.1 = (s32[24]{0:T(128)S(1)}, s32[24]{0:T(128)}, u32[]{:S(2)}) copy-start(s32[24]{0:T(128)} %refs_0_.3) | copy-start | bytes 292
  9.7 59.3 %all-to-all-start = ((f32[24,4,8,384]{3,2,1,0:T(8,128)}), f32[24,4,8,384]{3,2,1,0:T(8,128)S(1)}, u32[]{:S(2)}, u32[]{:S(2)}) async-start(f32[24,4,8,384]{3,2,1,0:T(8,128)} %copy_bitcast_fusion), calls=%async_computation | async-start | bytes 2359296 | tf_op jit(solution)/shard_map/all_to_all | solution.py:253
  29.8 208.4 %all-gather.7.cloned.1.call-start = ((), (), s32[]{:S(2)}) async-start(), calls=%async_computation.5 | async-start | bytes 5308416 | tf_op jit(solution)/shard_map/all_gather | solution.py:267
  70.1 44.2 %copy-start = (f32[2,1,192,384]{3,2,1,0:T(8,128)S(1)}, f32[2,1,192,384]{3,2,1,0:T(8,128)}, u32[]{:S(2)}) copy-start(f32[2,1,192,384]{3,2,1,0:T(8,128)} %param.4) | copy-start | bytes 1769476
  92.3 9.7 %collective-permute-start.5 = (f32[12,2,8,384]{3,2,1,0:T(8,128)S(1)}, f32[12,2,8,384]{3,2,1,0:T(8,128)S(1)}, u32[]{:S(2)}, u32[]{:S(2)}) collective-permute-start(f32[12,2,8,384]{3,2,1,0:T(8,128)S(1)} %get-tuple-element.15.refs_1_), channel_id=1, source_target_pairs={{0,8},{8,0},{16,24},{24,16},{1,9},{9,1},{17,25},{25,17},{2,10},{10... | collective-permute-start | bytes 884744 | tf_op jit(solution)/shard_map/ppermute | solution.py:219
  94.2 14.1 %collective-permute-start = (f32[12,2,8,384]{3,2,1,0:T(8,128)S(1)}, f32[12,2,8,384]{3,2,1,0:T(8,128)S(1)}, u32[]{:S(2)}, u32[]{:S(2)}) collective-permute-start(f32[12,2,8,384]{3,2,1,0:T(8,128)S(1)} %get-tuple-element.16.refs_1_), channel_id=1, source_target_pairs={{0,8},{8,0},{16,24},{24,16},{1,9},{9,1},{17,25},{25,17},{2,10},{10... | collective-permute-start | bytes 884744 | tf_op jit(solution)/shard_map/ppermute | solution.py:219
  97.6 11.4 %collective-permute-start.8 = (f32[12,2,8,384]{3,2,1,0:T(8,128)S(1)}, f32[12,2,8,384]{3,2,1,0:T(8,128)S(1)}, u32[]{:S(2)}, u32[]{:S(2)}) collective-permute-start(f32[12,2,8,384]{3,2,1,0:T(8,128)S(1)} %get-tuple-element.15.refs_1_), channel_id=1, source_target_pairs={{8,16},{16,8},{9,17},{17,9},{10,18},{18,10},{11,19},{19,11},{12,20... | collective-permute-start | bytes 884744 | tf_op jit(solution)/shard_map/ppermute | solution.py:219
  98.3 12.0 %collective-permute-start.3 = (f32[12,2,8,384]{3,2,1,0:T(8,128)S(1)}, f32[12,2,8,384]{3,2,1,0:T(8,128)S(1)}, u32[]{:S(2)}, u32[]{:S(2)}) collective-permute-start(f32[12,2,8,384]{3,2,1,0:T(8,128)S(1)} %get-tuple-element.16.refs_1_), channel_id=1, source_target_pairs={{8,16},{16,8},{9,17},{17,9},{10,18},{18,10},{11,19},{19,11},{12,20... | collective-permute-start | bytes 884744 | tf_op jit(solution)/shard_map/ppermute | solution.py:219
  102.0 9.6 %collective-permute-start.6 = (f32[12,2,8,384]{3,2,1,0:T(8,128)S(1)}, f32[12,2,8,384]{3,2,1,0:T(8,128)S(1)}, u32[]{:S(2)}, u32[]{:S(2)}) collective-permute-start(f32[12,2,8,384]{3,2,1,0:T(8,128)S(1)} %collective-permute-done.5.refs_3_), channel_id=1, source_target_pairs={{8,16},{16,8},{9,17},{17,9},{10,18},{18,10},{11,19},{19,11},{12,20... | collective-permute-start | bytes 884744 | tf_op jit(solution)/shard_map/ppermute | solution.py:219
  108.3 4.6 %collective-permute-start.1 = (f32[12,2,8,384]{3,2,1,0:T(8,128)S(1)}, f32[12,2,8,384]{3,2,1,0:T(8,128)S(1)}, u32[]{:S(2)}, u32[]{:S(2)}) collective-permute-start(f32[12,2,8,384]{3,2,1,0:T(8,128)S(1)} %collective-permute-done.refs_3_), channel_id=1, source_target_pairs={{8,16},{16,8},{9,17},{17,9},{10,18},{18,10},{11,19},{19,11},{12,20... | collective-permute-start | bytes 884744 | tf_op jit(solution)/shard_map/ppermute | solution.py:219
  109.0 28.6 %collective-permute-start.9 = (f32[12,2,8,384]{3,2,1,0:T(8,128)S(1)}, f32[12,2,8,384]{3,2,1,0:T(8,128)}, u32[]{:S(2)}, u32[]{:S(2)}) collective-permute-start(f32[12,2,8,384]{3,2,1,0:T(8,128)S(1)} %collective-permute-done.8.refs_1_), channel_id=1, source_target_pairs={{8,0},{16,24},{9,1},{17,25},{10,2},{18,26},{11,3},{19,27},{12,4},{... | collective-permute-start | bytes 884744 | tf_op jit(solution)/shard_map/ppermute | solution.py:219
  110.3 33.6 %collective-permute-start.4 = (f32[12,2,8,384]{3,2,1,0:T(8,128)S(1)}, f32[12,2,8,384]{3,2,1,0:T(8,128)}, u32[]{:S(2)}, u32[]{:S(2)}) collective-permute-start(f32[12,2,8,384]{3,2,1,0:T(8,128)S(1)} %collective-permute-done.3.refs_1_), channel_id=1, source_target_pairs={{8,0},{16,24},{9,1},{17,25},{10,2},{18,26},{11,3},{19,27},{12,4},{... | collective-permute-start | bytes 884744 | tf_op jit(solution)/shard_map/ppermute | solution.py:219
  111.6 38.6 %collective-permute-start.7 = (f32[12,2,8,384]{3,2,1,0:T(8,128)S(1)}, f32[12,2,8,384]{3,2,1,0:T(8,128)}, u32[]{:S(2)}, u32[]{:S(2)}) collective-permute-start(f32[12,2,8,384]{3,2,1,0:T(8,128)S(1)} %collective-permute-done.6.refs_1_), channel_id=1, source_target_pairs={{8,0},{16,24},{9,1},{17,25},{10,2},{18,26},{11,3},{19,27},{12,4},{... | collective-permute-start | bytes 884744 | tf_op jit(solution)/shard_map/ppermute | solution.py:219
  112.9 43.6 %collective-permute-start.2 = (f32[12,2,8,384]{3,2,1,0:T(8,128)S(1)}, f32[12,2,8,384]{3,2,1,0:T(8,128)}, u32[]{:S(2)}, u32[]{:S(2)}) collective-permute-start(f32[12,2,8,384]{3,2,1,0:T(8,128)S(1)} %collective-permute-done.1.refs_1_), channel_id=1, source_target_pairs={{8,0},{16,24},{9,1},{17,25},{10,2},{18,26},{11,3},{19,27},{12,4},{... | collective-permute-start | bytes 884744 | tf_op jit(solution)/shard_map/ppermute | solution.py:219
  208.0 17.8 %collective-permute-start.15 = (f32[12,2,8,384]{3,2,1,0:T(8,128)S(1)}, f32[12,2,8,384]{3,2,1,0:T(8,128)S(1)}, u32[]{:S(2)}, u32[]{:S(2)}) collective-permute-start(f32[12,2,8,384]{3,2,1,0:T(8,128)S(1)} %get-tuple-element.13.refs_1_), channel_id=1, source_target_pairs={{0,8},{8,0},{16,24},{24,16},{1,9},{9,1},{17,25},{25,17},{2,10},{10... | collective-permute-start | bytes 884744 | tf_op jit(solution)/shard_map/ppermute | solution.py:219
  219.2 12.9 %collective-permute-start.10 = (f32[12,2,8,384]{3,2,1,0:T(8,128)S(1)}, f32[12,2,8,384]{3,2,1,0:T(8,128)S(1)}, u32[]{:S(2)}, u32[]{:S(2)}) collective-permute-start(f32[12,2,8,384]{3,2,1,0:T(8,128)S(1)} %get-tuple-element.14.refs_1_), channel_id=1, source_target_pairs={{0,8},{8,0},{16,24},{24,16},{1,9},{9,1},{17,25},{25,17},{2,10},{10... | collective-permute-start | bytes 884744 | tf_op jit(solution)/shard_map/ppermute | solution.py:219
  221.2 11.6 %collective-permute-start.18 = (f32[12,2,8,384]{3,2,1,0:T(8,128)S(1)}, f32[12,2,8,384]{3,2,1,0:T(8,128)S(1)}, u32[]{:S(2)}, u32[]{:S(2)}) collective-permute-start(f32[12,2,8,384]{3,2,1,0:T(8,128)S(1)} %get-tuple-element.13.refs_1_), channel_id=1, source_target_pairs={{8,16},{16,8},{9,17},{17,9},{10,18},{18,10},{11,19},{19,11},{12,20... | collective-permute-start | bytes 884744 | tf_op jit(solution)/shard_map/ppermute | solution.py:219
  225.8 8.3 %collective-permute-start.16 = (f32[12,2,8,384]{3,2,1,0:T(8,128)S(1)}, f32[12,2,8,384]{3,2,1,0:T(8,128)S(1)}, u32[]{:S(2)}, u32[]{:S(2)}) collective-permute-start(f32[12,2,8,384]{3,2,1,0:T(8,128)S(1)} %collective-permute-done.15.refs_3_), channel_id=1, source_target_pairs={{8,16},{16,8},{9,17},{17,9},{10,18},{18,10},{11,19},{19,11},{12,20... | collective-permute-start | bytes 884744 | tf_op jit(solution)/shard_map/ppermute | solution.py:219
  226.5 8.9 %collective-permute-start.13 = (f32[12,2,8,384]{3,2,1,0:T(8,128)S(1)}, f32[12,2,8,384]{3,2,1,0:T(8,128)S(1)}, u32[]{:S(2)}, u32[]{:S(2)}) collective-permute-start(f32[12,2,8,384]{3,2,1,0:T(8,128)S(1)} %get-tuple-element.14.refs_1_), channel_id=1, source_target_pairs={{8,16},{16,8},{9,17},{17,9},{10,18},{18,10},{11,19},{19,11},{12,20... | collective-permute-start | bytes 884744 | tf_op jit(solution)/shard_map/ppermute | solution.py:219
  232.1 4.6 %collective-permute-start.11 = (f32[12,2,8,384]{3,2,1,0:T(8,128)S(1)}, f32[12,2,8,384]{3,2,1,0:T(8,128)S(1)}, u32[]{:S(2)}, u32[]{:S(2)}) collective-permute-start(f32[12,2,8,384]{3,2,1,0:T(8,128)S(1)} %collective-permute-done.10.refs_3_), channel_id=1, source_target_pairs={{8,16},{16,8},{9,17},{17,9},{10,18},{18,10},{11,19},{19,11},{12,20... | collective-permute-start | bytes 884744 | tf_op jit(solution)/shard_map/ppermute | solution.py:219
  232.8 12.0 %collective-permute-start.19 = (f32[12,2,8,384]{3,2,1,0:T(8,128)S(1)}, f32[12,2,8,384]{3,2,1,0:T(8,128)}, u32[]{:S(2)}, u32[]{:S(2)}) collective-permute-start(f32[12,2,8,384]{3,2,1,0:T(8,128)S(1)} %collective-permute-done.18.refs_1_), channel_id=1, source_target_pairs={{8,0},{16,24},{9,1},{17,25},{10,2},{18,26},{11,3},{19,27},{12,4},{... | collective-permute-start | bytes 884744 | tf_op jit(solution)/shard_map/ppermute | solution.py:219
  234.1 13.7 %collective-permute-start.17 = (f32[12,2,8,384]{3,2,1,0:T(8,128)S(1)}, f32[12,2,8,384]{3,2,1,0:T(8,128)}, u32[]{:S(2)}, u32[]{:S(2)}) collective-permute-start(f32[12,2,8,384]{3,2,1,0:T(8,128)S(1)} %collective-permute-done.16.refs_1_), channel_id=1, source_target_pairs={{8,0},{16,24},{9,1},{17,25},{10,2},{18,26},{11,3},{19,27},{12,4},{... | collective-permute-start | bytes 884744 | tf_op jit(solution)/shard_map/ppermute | solution.py:219
  235.4 18.7 %collective-permute-start.14 = (f32[12,2,8,384]{3,2,1,0:T(8,128)S(1)}, f32[12,2,8,384]{3,2,1,0:T(8,128)S(1)}, u32[]{:S(2)}, u32[]{:S(2)}) collective-permute-start(f32[12,2,8,384]{3,2,1,0:T(8,128)S(1)} %collective-permute-done.13.refs_1_), channel_id=1, source_target_pairs={{8,0},{16,24},{9,1},{17,25},{10,2},{18,26},{11,3},{19,27},{12,4},{... | collective-permute-start | bytes 884744 | tf_op jit(solution)/shard_map/ppermute | solution.py:219
  236.7 23.6 %collective-permute-start.12 = (f32[12,2,8,384]{3,2,1,0:T(8,128)S(1)}, f32[12,2,8,384]{3,2,1,0:T(8,128)S(1)}, u32[]{:S(2)}, u32[]{:S(2)}) collective-permute-start(f32[12,2,8,384]{3,2,1,0:T(8,128)S(1)} %collective-permute-done.11.refs_1_), channel_id=1, source_target_pairs={{8,0},{16,24},{9,1},{17,25},{10,2},{18,26},{11,3},{19,27},{12,4},{... | collective-permute-start | bytes 884744 | tf_op jit(solution)/shard_map/ppermute | solution.py:219
Sparse Core Ops, SparseCore 0:
  9.7 50.2 all-gather.4
  159.5 36.1 all-gather.6
